TPU v7x, 256 devices: a whole 4x4x8 slice. The times are simulated.
256 devices in a mesh: seq: 64 (over x, z_hi, y), dp: 4 (over z_lo, core).
Axes of the slice: x: 4, y: 4, z: 8 (z_hi: 4, z_lo: 2; z = z_hi * 2 + z_lo), core: 2. Of those that a mesh axis runs over, the one named last changes fastest.
Arguments:
- tokens: bfloat16 [32768, 1024], P(('dp', 'seq')), parts along dimension 0, may hold values from -6 to 6
- norm_gain: float32 [1024], replicated, may hold values from 0.1 to 1.9
- filters: float32 [12, 8192], P(None, 'seq'), may hold values from -0.0625 to 0.0625
- mixing: bfloat16 [12, 1024, 1024], P(None, 'seq'), may hold values from -0.0546875 to 0.0546875
Outputs:
- mixed: bfloat16 [32768, 1024], P(('dp', 'seq')), parts along dimension 0
There are 4 independent parts, one for each index of `dp`. A program takes and returns all parts, laid end to end along the dimension named above; an argument that names none is the same for every part. Nothing has to cross between parts.
All inputs are finite; a program needn't handle non-finite values.
Results may differ from a plain program's by a relative error of at most 0.0044.
Values may be sent and summed in bfloat16 or wider, within the bound.
A program may use at most 192 MiB of HBM per device.

v0:
```python
import math
import jax
import jax.numpy as jnp
from jax import lax
from jax.sharding import PartitionSpec as P

radix = 128
highest = lax.Precision.HIGHEST


def cos_sin(rows, cols, total):
    left = lax.broadcasted_iota(jnp.int32, (rows, cols), 0)
    right = lax.broadcasted_iota(jnp.int32, (rows, cols), 1)
    angle = (left * right % total).astype(jnp.float32) * (2.0 * math.pi / total)
    return (jnp.cos(angle), jnp.sin(angle))


def make_tables(blocks):
    total = blocks * radix
    half = blocks // 2
    cos_outer, sin_outer = cos_sin(blocks, half, blocks)
    cos_twid, sin_twid = cos_sin(blocks, radix, total)
    cos_inner, sin_inner = cos_sin(radix, radix, radix)
    cos_back, sin_back = cos_sin(half, blocks, blocks)
    return (
        cos_outer,
        sin_outer,
        cos_twid,
        sin_twid,
        cos_inner,
        sin_inner,
        cos_back,
        sin_back,
        total,
    )


def forward(signal, tables):
    cos_outer, sin_outer, cos_twid, sin_twid, cos_inner, sin_inner, cos_back, sin_back, total = (
        tables
    )
    first_re = jnp.einsum("kn,cna->cka", cos_outer, signal, precision=highest)
    first_im = -jnp.einsum("kn,cna->cka", sin_outer, signal, precision=highest)
    twist_re = first_re * cos_twid + first_im * sin_twid
    twist_im = first_im * cos_twid - first_re * sin_twid
    out_re = jnp.einsum("cka,aj->ckj", twist_re, cos_inner, precision=highest) + jnp.einsum(
        "cka,aj->ckj", twist_im, sin_inner, precision=highest
    )
    out_im = jnp.einsum("cka,aj->ckj", twist_im, cos_inner, precision=highest) - jnp.einsum(
        "cka,aj->ckj", twist_re, sin_inner, precision=highest
    )
    return (out_re, out_im)


def inverse(spec_re, spec_im, tables):
    cos_outer, sin_outer, cos_twid, sin_twid, cos_inner, sin_inner, cos_back, sin_back, total = (
        tables
    )
    inner_re = jnp.einsum("ckj,aj->cka", spec_re, cos_inner, precision=highest) - jnp.einsum(
        "ckj,aj->cka", spec_im, sin_inner, precision=highest
    )
    inner_im = jnp.einsum("ckj,aj->cka", spec_im, cos_inner, precision=highest) + jnp.einsum(
        "ckj,aj->cka", spec_re, sin_inner, precision=highest
    )
    twist_re = inner_re * cos_twid - inner_im * sin_twid
    twist_im = inner_im * cos_twid + inner_re * sin_twid
    result = jnp.einsum("nk,cka->cna", cos_back, twist_re, precision=highest) - jnp.einsum(
        "nk,cka->cna", sin_back, twist_im, precision=highest
    )
    return result / total


def local(tokens, norm_gain, filters, mixing):
    tok_rows, width = tokens.shape
    groups = lax.axis_size("seq")
    values = tokens.astype(jnp.float32)
    scale_row = lax.rsqrt(jnp.mean(values * values, axis=1, keepdims=True) + 1e-05)
    normed = (values * scale_row * norm_gain).astype(jnp.bfloat16)
    taps = lax.all_gather(filters, "seq", axis=1, tiled=True)
    num_filters, length = taps.shape
    blocks = 2 * length // radix
    half = blocks // 2
    tables = make_tables(blocks)
    phi_re, phi_im = forward(taps.reshape(num_filters, half, radix), tables)
    grouped = normed.reshape(tok_rows, groups, width // groups)
    piece = lax.all_to_all(grouped, "seq", split_axis=1, concat_axis=0, tiled=True)
    count = piece.shape[2]
    signal = piece[:, 0, :].astype(jnp.float32).T.reshape(count, half, radix)
    sig_re, sig_im = forward(signal, tables)

    def per_filter(spectrum):
        filt_re, filt_im = spectrum
        prod_re = sig_re * filt_re - sig_im * filt_im
        prod_im = sig_re * filt_im + sig_im * filt_re
        return inverse(prod_re, prod_im, tables).reshape(count, length).astype(jnp.bfloat16)

    features = lax.map(per_filter, (phi_re, phi_im))
    back = lax.all_to_all(features, "seq", split_axis=2, concat_axis=1, tiled=True)
    branch = jnp.einsum(
        "kct,kcd->td",
        back,
        lax.all_gather(mixing, "seq", axis=1, tiled=True),
        preferred_element_type=jnp.float32,
    )
    return (values + branch).astype(jnp.bfloat16)


def solution(mesh):
    in_specs = (P(("dp", "seq"), None), P(), P(None, "seq"), P(None, "seq", None))
    out_specs = P(("dp", "seq"), None)
    return jax.shard_map(local, mesh=mesh, in_specs=in_specs, out_specs=out_specs, check_vma=False)
```

profile of v0, /device:TPU:32, one launch (start us, length us, event | category | flops | bytes accessed | tf_op | source)
XLA Modules:
  0.0 559.1 jit_solution(12533361922189063383)
XLA Ops:
  10.3 13.7 %all-to-all-start = ((bf16[128,64,16]{0,2,1:T(8,128)(2,1)}), bf16[128,64,16]{0,2,1:T(8,128)(2,1)S(1)}, u32[]{:S(2)}, u32[]{:S(2)}) async-start(bf16[128,64,16]{0,2,1:T(8,128)(2,1)} %bitcast.6), calls=%async_computation | async-start | bytes 524288 | tf_op jit(solution)/shard_map/all_to_all | solution.py:86
  24.4 222.2 %all_gather.6 = f32[12,8192]{1,0:T(8,128)S(1)} all-gather(f32[12,128]{1,0:T(8,128)} %param.8), channel_id=1, replica_groups=mesh['seq'=64,'dp'=4] {'seq'}, dimensions={1}, use_global_device_ids=true | all-gather | bytes 399360 | tf_op jit(solution)/shard_map/all_gather | solution.py:79
  251.8 1.9 convolution_add_fusion.2
  255.5 2.0 fusion.102
  257.5 2.2 fusion.103
  259.7 2.0 convolution_add_fusion.1
  261.7 2.0 convolution_subtract_fusion.2
  263.7 106.2 %while.12 = (s32[]{:T(128)}, bf16[12,16,8192]{2,1,0:T(8,128)(2,1)}, f32[12,128,128]{2,1,0:T(8,128)}, f32[16,128,128]{2,1,0:T(8,128)S(1)}, f32[12,128,128]{2,1,0:...) while((s32[]{:T(128)}, bf16[12,16,8192]{2,1,0:T(8,128)(2,1)}, ...), condition=%wide.region_2.3_spmd.clone.clone, body=%wide.region_1.2_spmd.clone.clone.sunk | while | flops 2020278272 | bytes 22413904 | solution.py:97
  264.6 1.2 fusion.225
  273.4 1.2 fusion.225
  275.9 1.2 fusion.224
  282.3 1.2 fusion.225
  284.8 1.2 fusion.224
  293.6 1.2 fusion.224
  302.5 1.2 fusion.224
  311.3 1.2 fusion.224
  320.2 1.2 fusion.224
  326.5 1.2 fusion.225
  329.0 1.2 fusion.224
  335.4 1.2 fusion.225
  337.9 1.2 fusion.224
  344.2 1.2 fusion.225
  353.1 1.2 fusion.225
  355.6 1.2 fusion.224
  361.9 1.2 fusion.225
  364.4 1.2 fusion.224
  369.9 27.1 %copy.39 = bf16[12,16,8192]{1,0,2:T(8,128)(2,1)} copy(bf16[12,16,8192]{2,1,0:T(8,128)(2,1)} %get-tuple-element.79) | data formatting | bytes 6291456 | tf_op jit(solution)/shard_map/while | solution.py:97
  397.0 34.7 %reshape.71 = bf16[64,2,12288]{2,1,0:T(2,128)(2,1)S(1)} reshape(bf16[8192,12,16]{2,1,0:T(8,128)(2,1)} %bitcast.116) | data formatting | bytes 6291456
  431.7 46.9 %all_to_all.33 = bf16[64,2,12288]{2,1,0:T(2,128)(2,1)} all-to-all(bf16[64,2,12288]{2,1,0:T(2,128)(2,1)S(1)} %reshape.71), channel_id=1, replica_groups=mesh['seq'=64,'dp'=4] {'seq'}, dimensions={0} | all-to-all | bytes 6291456 | tf_op jit(solution)/shard_map/all_to_all | solution.py:98
  478.6 34.0 %reshape.72 = bf16[8192,12,16]{2,1,0:T(8,128)(2,1)} reshape(bf16[64,2,12288]{2,1,0:T(2,128)(2,1)} %all_to_all.33) | data formatting | bytes 6291456
  512.6 28.9 %copy.41 = bf16[12,64,16,128]{3,2,1,0:T(8,128)(2,1)S(1)} copy(bf16[12,64,16,128]{2,0,3,1:T(8,128)(2,1)} %bitcast.117) | data formatting | bytes 6291456 | tf_op jit(solution)/shard_map/all_to_all | solution.py:98
  541.5 10.7 %fusion.89 = bf16[128,1024]{1,0:T(8,128)(2,1)} fusion(bf16[12,1024,128]{2,1,0:T(8,128)(2,1)S(1)} %bitcast.118, bf16[12,1024,1024]{2,1,0:T(8,128)(2,1)} %all-gather.2.cloned.1.call-done, bf16[128,1024]{1,0:T(8,128)(2,1)S(1)} %copy-done), kind=kOutput, calls=%fused_computation.102 | convolution fusion | flops 3221618688 | bytes 28835840 | tf_op jit(solution)/shard_map/kct,kcd->td/dot_general | solution.py:99
  (127 shorter events, 94.2 us)
Async XLA Ops:
  6.5 535.0 %all-gather.2.cloned.1.call-start = ((), (), s32[]{:S(2)}) async-start(), calls=%async_computation.2 | async-start | bytes 25559040 | tf_op jit(solution)/shard_map/all_gather | solution.py:102
  10.3 243.4 %all-to-all-start = ((bf16[128,64,16]{0,2,1:T(8,128)(2,1)}), bf16[128,64,16]{0,2,1:T(8,128)(2,1)S(1)}, u32[]{:S(2)}, u32[]{:S(2)}) async-start(bf16[128,64,16]{0,2,1:T(8,128)(2,1)} %bitcast.6), calls=%async_computation | async-start | bytes 524288 | tf_op jit(solution)/shard_map/all_to_all | solution.py:86
  512.6 28.9 %copy-start = (bf16[128,1024]{1,0:T(8,128)(2,1)S(1)}, bf16[128,1024]{1,0:T(8,128)(2,1)}, u32[]{:S(2)}) copy-start(bf16[128,1024]{1,0:T(8,128)(2,1)} %param.6) | copy-start | bytes 786436
Sparse Core Ops, SparseCore 0:
  10.7 238.2 all-gather.1
where the time goes:
time: 563 us; the launch traced here: 559 us
  blocking collectives  269 us (48%)
  local copies, waits for them, and re-layouts  146 us (26%)
  matrix products  109 us (19%)
  starting transfers between devices  13.7 us (2%)
  between operations  13.6 us (2%)
  other arithmetic  5.77 us (1%)
    all_gather x1, blocking collectives, local(): taps = lax.all_gather(filters, 'seq', axis=1, tiled=True)  222 us
    unnamed x7, local copies, waits for them, and re-layouts  69 us
    all_to_all x1, blocking collectives, local(): lax.all_to_all(features, 'seq', split_axis=2, concat_axis=1, tiled=True)  46.9 us
    all_to_all x1, local copies, waits for them, and re-layouts, local(): lax.all_to_all(features, 'seq', split_axis=2, concat_axis=1, tiled=True)  28.9 us
    while x1, local copies, waits for them, and re-layouts, local(): features = lax.map(per_filter, (phi_re, phi_im))  27.1 us
    dot_general x12, matrix products, inverse(): jnp.einsum('ckj,aj->cka', spec_im, cos_inner, precision=highest)  14.9 us
    dot_general x12, matrix products, inverse(): jnp.einsum('ckj,aj->cka', spec_re, cos_inner, precision=highest)  14.9 us
    dot_general x12, matrix products, inverse(): jnp.einsum('ckj,aj->cka', spec_im, sin_inner, precision=highest)  14.8 us
  transfers between devices with their start and end apart: 2, of which 0 were waited for; matrix products, arithmetic and copies ran while one was open for 45% of the time, Pallas kernels for 0%

commit v1 on v0

--- a/solution.py
+++ b/solution.py
@@ -6,6 +6,12 @@
 
 radix = 128
 highest = lax.Precision.HIGHEST
+
+
+def stacked_exchange(value, axis, split, join):
+    pieces = jnp.split(value, lax.axis_size(axis), axis=split)
+    incoming = lax.all_to_all(jnp.stack(pieces), axis, 0, 0)
+    return jnp.concatenate(incoming, axis=join)
 
 
 def cos_sin(rows, cols, total):
@@ -95,7 +101,7 @@
         return inverse(prod_re, prod_im, tables).reshape(count, length).astype(jnp.bfloat16)
 
     features = lax.map(per_filter, (phi_re, phi_im))
-    back = lax.all_to_all(features, "seq", split_axis=2, concat_axis=1, tiled=True)
+    back = stacked_exchange(features, "seq", 2, 1)
     branch = jnp.einsum(
         "kct,kcd->td",
         back,

time: 563 us -> 473 us (0.84)
  local copies, waits for them, and re-layouts: 146 us -> 49.4 us
  blocking collectives: 269 us -> 278 us
    unnamed x7 -> x70, local copies, waits for them, and re-layouts: 69 us -> 27.2 us
    all_to_all x1, local copies, waits for them, and re-layouts: 28.9 us -> 0.73 us  [stacked_exchange(): incoming = lax.all_to_all(jnp.stack(pieces), axis, 0, 0)]
    while x1 -> x0, local copies, waits for them, and re-layouts: 27.1 us -> none  [local(): features = lax.map(per_filter, (phi_re, phi_im))]
    all_to_all x1, blocking collectives: 46.9 us -> 64.6 us  [stacked_exchange(): incoming = lax.all_to_all(jnp.stack(pieces), axis, 0, 0)]
    all_gather x1, blocking collectives: 222 us -> 213 us  [local(): taps = lax.all_gather(filters, 'seq', axis=1, tiled=True)]
  transfers between devices with their start and end apart: 2 -> 2, of which waited for: 0 -> 0; matrix products, arithmetic and copies ran while one was open for 45% -> 32% of each run, Pallas kernels for 0% -> 0%
where the time goes in v1:
time: 473 us; the launch traced here: 471 us
  blocking collectives  278 us (59%)
  matrix products  109 us (23%)
  local copies, waits for them, and re-layouts  49.4 us (10%)
  starting transfers between devices  13.7 us (3%)
  between operations  13.7 us (3%)
  other arithmetic  5.77 us (1%)
    all_gather x1, blocking collectives, local(): taps = lax.all_gather(filters, 'seq', axis=1, tiled=True)  213 us
    all_to_all x1, blocking collectives, stacked_exchange(): incoming = lax.all_to_all(jnp.stack(pieces), axis, 0, 0)  64.6 us
    unnamed x70, local copies, waits for them, and re-layouts  27.2 us
    dot_general x12, matrix products, inverse(): jnp.einsum('ckj,aj->cka', spec_im, cos_inner, precision=highest)  14.9 us
    dot_general x12, matrix products, inverse(): jnp.einsum('ckj,aj->cka', spec_im, sin_inner, precision=highest)  14.9 us
    dot_general x12, matrix products, inverse(): jnp.einsum('ckj,aj->cka', spec_re, sin_inner, precision=highest)  14.8 us
    dot_general x12, matrix products, inverse(): jnp.einsum('ckj,aj->cka', spec_re, cos_inner, precision=highest)  14.8 us
    all_to_all x1, starting transfers between devices, local(): lax.all_to_all(grouped, 'seq', split_axis=1, concat_axis=0, tiled=True)  13.7 us
  transfers between devices with their start and end apart: 2, of which 0 were waited for; matrix products, arithmetic and copies ran while one was open for 32% of the time, Pallas kernels for 0%

profile of v1, /device:TPU:32, one launch (start us, length us, event | category | flops | bytes accessed | tf_op | source)
XLA Modules:
  0.0 470.8 jit_solution(14988345715707751712)
XLA Ops:
  9.6 13.7 %all-to-all-start = ((bf16[128,64,16]{0,2,1:T(8,128)(2,1)}), bf16[128,64,16]{0,2,1:T(8,128)(2,1)S(1)}, u32[]{:S(2)}, u32[]{:S(2)}) async-start(bf16[128,64,16]{0,2,1:T(8,128)(2,1)} %bitcast.6), calls=%async_computation | async-start | bytes 524288 | tf_op jit(solution)/shard_map/all_to_all | solution.py:92
  24.3 212.9 %all_gather.6 = f32[12,8192]{1,0:T(8,128)S(1)} all-gather(f32[12,128]{1,0:T(8,128)} %param.8), channel_id=1, replica_groups=mesh['seq'=64,'dp'=4] {'seq'}, dimensions={1}, use_global_device_ids=true | all-gather | bytes 399360 | tf_op jit(solution)/shard_map/all_gather | solution.py:85
  242.5 1.9 convolution_add_fusion.2
  246.2 2.0 fusion.102
  248.2 2.2 fusion.103
  250.4 2.0 convolution_add_fusion.1
  252.4 2.0 convolution_subtract_fusion.2
  254.4 106.3 %while.12 = (s32[]{:T(128)}, bf16[12,16,8192]{2,1,0:T(8,128)(2,1)}, f32[12,128,128]{2,1,0:T(8,128)}, f32[16,128,128]{2,1,0:T(8,128)S(1)}, f32[12,128,128]{2,1,0:...) while((s32[]{:T(128)}, bf16[12,16,8192]{2,1,0:T(8,128)(2,1)}, ...), condition=%wide.region_2.3_spmd.clone.clone, body=%wide.region_1.2_spmd.clone.clone.sunk | while | flops 2020278272 | bytes 22413904 | solution.py:103
  264.2 1.2 fusion.225
  265.4 1.2 convolution_subtract_fusion.5
  266.7 1.2 fusion.224
  274.3 1.2 convolution_subtract_fusion.5
  275.5 1.2 fusion.224
  281.9 1.2 fusion.225
  284.4 1.2 fusion.224
  285.7 1.2 convolution_add_fusion.4
  294.5 1.2 convolution_add_fusion.4
  299.6 1.2 fusion.225
  302.1 1.2 fusion.224
  311.0 1.2 fusion.224
  319.8 1.2 fusion.224
  321.1 1.2 convolution_add_fusion.4
  327.4 1.2 convolution_subtract_fusion.5
  328.7 1.2 fusion.224
  335.0 1.2 fusion.225
  336.3 1.2 convolution_subtract_fusion.5
  337.5 1.2 fusion.224
  346.4 1.2 fusion.224
  352.7 1.2 fusion.225
  355.2 1.2 fusion.224
  387.6 64.6 %all_to_all.20 = bf16[64,12,16,128]{3,2,1,0:T(8,128)(2,1)S(1)} all-to-all(bf16[64,12,16,128]{3,2,1,0:T(8,128)(2,1)S(1)} %constant_dynamic-update-slice_fusion.1), channel_id=1, replica_groups=mesh['seq'=64,'dp'=4] {'seq'}, dimensions={0} | all-to-all | bytes 6291456 | tf_op jit(solution)/shard_map/all_to_all | solution.py:13
  453.2 10.7 %fusion.89 = bf16[128,1024]{1,0:T(8,128)(2,1)} fusion(bf16[12,1024,128]{2,1,0:T(8,128)(2,1)S(1)} %bitcast.240, bf16[12,1024,1024]{2,1,0:T(8,128)(2,1)} %all-gather.2.cloned.1.call-done, bf16[128,1024]{1,0:T(8,128)(2,1)S(1)} %copy-done.1), kind=kOutput, calls=%fused_computation.102 | convolution fusion | flops 3221618688 | bytes 28835840 | tf_op jit(solution)/shard_map/kct,kcd->td/dot_general | solution.py:105
  (190 shorter events, 117.0 us)
Async XLA Ops:
  9.6 234.9 %all-to-all-start = ((bf16[128,64,16]{0,2,1:T(8,128)(2,1)}), bf16[128,64,16]{0,2,1:T(8,128)(2,1)S(1)}, u32[]{:S(2)}, u32[]{:S(2)}) async-start(bf16[128,64,16]{0,2,1:T(8,128)(2,1)} %bitcast.6), calls=%async_computation | async-start | bytes 524288 | tf_op jit(solution)/shard_map/all_to_all | solution.py:92
  23.2 429.8 %all-gather.2.cloned.1.call-start = ((), (), s32[]{:S(2)}) async-start(), calls=%async_computation.2 | async-start | bytes 25559040 | tf_op jit(solution)/shard_map/all_gather | solution.py:108
  360.8 26.0 %copy-start = (bf16[12,16,8192]{2,1,0:T(8,128)(2,1)S(1)}, bf16[12,16,8192]{2,1,0:T(8,128)(2,1)}, u32[]{:S(2)}) copy-start(bf16[12,16,8192]{2,1,0:T(8,128)(2,1)} %get-tuple-element.79) | copy-start | bytes 9437188
  452.2 1.0 copy-start.1
Sparse Core Ops, SparseCore 0:
  27.4 239.3 all-gather.1

commit v2 on v0

--- a/solution.py
+++ b/solution.py
@@ -6,6 +6,13 @@
 
 radix = 128
 highest = lax.Precision.HIGHEST
+
+
+def swapped_in(x, name, dim):
+    size = lax.axis_size(name)
+    blocks = jnp.stack([x for _ in range(size)])
+    blocks = lax.all_to_all(blocks, name, split_axis=0, concat_axis=0)
+    return jnp.concatenate(blocks, axis=dim)
 
 
 def cos_sin(rows, cols, total):
@@ -76,7 +83,7 @@
     values = tokens.astype(jnp.float32)
     scale_row = lax.rsqrt(jnp.mean(values * values, axis=1, keepdims=True) + 1e-05)
     normed = (values * scale_row * norm_gain).astype(jnp.bfloat16)
-    taps = lax.all_gather(filters, "seq", axis=1, tiled=True)
+    taps = swapped_in(filters, "seq", 1)
     num_filters, length = taps.shape
     blocks = 2 * length // radix
     half = blocks // 2

time: 563 us -> 406 us (0.72)
  blocking collectives: 269 us -> 71.3 us
  waiting for transfers between devices: 0.73 us -> 34.5 us
    all_gather x1 -> x0, blocking collectives: 222 us -> none  [local(): taps = lax.all_gather(filters, 'seq', axis=1, tiled=True)]
    all_to_all x1, blocking collectives: 46.9 us -> 71.3 us  [local(): lax.all_to_all(features, 'seq', split_axis=2, concat_axis=1, tiled=True)]
    all_to_all x0 -> x1, waiting for transfers between devices: none -> 17 us  [swapped_in(): blocks = lax.all_to_all(blocks, name, split_axis=0, concat_axis=0)]
    all_to_all x1, waiting for transfers between devices: 0.01 us -> 16.8 us  [local(): lax.all_to_all(grouped, 'seq', split_axis=1, concat_axis=0, tiled=True)]
    unnamed x7 -> x6, local copies, waits for them, and re-layouts: 69 us -> 69 us
  transfers between devices with their start and end apart: 2 -> 3, of which waited for: 0 -> 2; matrix products, arithmetic and copies ran while one was open for 45% -> 63% of each run, Pallas kernels for 0% -> 0%
where the time goes in v2:
time: 406 us; the launch traced here: 402 us
  local copies, waits for them, and re-layouts  148 us (36%)
  matrix products  109 us (27%)
  blocking collectives  71.3 us (18%)
  waiting for transfers between devices  34.5 us (8%)
  starting transfers between devices  19.2 us (5%)
  between operations  13.6 us (3%)
  other arithmetic  5.77 us (1%)
    all_to_all x1, blocking collectives, local(): lax.all_to_all(features, 'seq', split_axis=2, concat_axis=1, tiled=True)  71.3 us
    unnamed x6, local copies, waits for them, and re-layouts  69 us
    all_to_all x1, local copies, waits for them, and re-layouts, local(): lax.all_to_all(features, 'seq', split_axis=2, concat_axis=1, tiled=True)  28.9 us
    while x1, local copies, waits for them, and re-layouts, local(): features = lax.map(per_filter, (phi_re, phi_im))  27.1 us
    all_to_all x1, waiting for transfers between devices, swapped_in(): blocks = lax.all_to_all(blocks, name, split_axis=0, concat_axis=0)  17 us
    all_to_all x1, waiting for transfers between devices, local(): lax.all_to_all(grouped, 'seq', split_axis=1, concat_axis=0, tiled=True)  16.8 us
    dot_general x12, matrix products, inverse(): jnp.einsum('ckj,aj->cka', spec_im, cos_inner, precision=highest)  14.9 us
    dot_general x12, matrix products, inverse(): jnp.einsum('ckj,aj->cka', spec_im, sin_inner, precision=highest)  14.9 us
  transfers between devices with their start and end apart: 3, of which 2 were waited for; matrix products, arithmetic and copies ran while one was open for 63% of the time, Pallas kernels for 0%

profile of v2, /device:TPU:32, one launch (start us, length us, event | category | flops | bytes accessed | tf_op | source)
XLA Modules:
  0.0 402.2 jit_solution(4407237507564421534)
XLA Ops:
  10.3 13.7 %all-to-all-start.1 = ((bf16[128,64,16]{0,2,1:T(8,128)(2,1)}), bf16[128,64,16]{0,2,1:T(8,128)(2,1)S(1)}, u32[]{:S(2)}, u32[]{:S(2)}) async-start(bf16[128,64,16]{0,2,1:T(8,128)(2,1)} %bitcast.7), calls=%async_computation.1 | async-start | bytes 524288 | tf_op jit(solution)/shard_map/all_to_all | solution.py:93
  24.4 16.8 %all-to-all-done.1 = bf16[128,64,16]{0,2,1:T(8,128)(2,1)S(1)} async-done(((bf16[128,64,16]{0,2,1:T(8,128)(2,1)}), bf16[128,64,16]{0,2,1:T(8,128)(2,1)S(1)}, u32[]{:S(2)}, u32[]{:S(2)}) %all-to-all-start.1) | async-done | bytes 262176 | tf_op jit(solution)/shard_map/all_to_all | solution.py:93
  41.2 1.5 stack.2
  42.7 5.5 %all-to-all-start = ((f32[64,12,128]{2,1,0:T(8,128)}), f32[64,12,128]{2,1,0:T(8,128)S(1)}, u32[]{:S(2)}, u32[]{:S(2)}) async-start(f32[64,12,128]{2,1,0:T(8,128)} %stack.2), calls=%async_computation | async-start | bytes 1048576 | tf_op jit(solution)/shard_map/all_to_all | solution.py:14
  50.0 2.0 fusion.104
  52.1 2.0 fusion.105
  54.1 2.0 convolution_add_fusion.1
  56.1 2.0 convolution_subtract_fusion.2
  58.1 17.0 %all-to-all-done = f32[64,12,128]{2,1,0:T(8,128)S(1)} async-done(((f32[64,12,128]{2,1,0:T(8,128)}), f32[64,12,128]{2,1,0:T(8,128)S(1)}, u32[]{:S(2)}, u32[]{:S(2)}) %all-to-all-start) | async-done | bytes 393248 | tf_op jit(solution)/shard_map/all_to_all | solution.py:14
  77.0 1.2 fusion.90
  80.3 1.9 convolution_add_fusion.2
  82.2 106.2 %while.12 = (s32[]{:T(128)}, bf16[12,16,8192]{2,1,0:T(8,128)(2,1)}, f32[12,128,128]{2,1,0:T(8,128)}, f32[16,128,128]{2,1,0:T(8,128)S(1)}, f32[12,128,128]{2,1,0:...) while((s32[]{:T(128)}, bf16[12,16,8192]{2,1,0:T(8,128)(2,1)}, ...), condition=%wide.region_2.3_spmd.clone.clone, body=%wide.region_1.2_spmd.clone.clone.sunk | while | flops 2020278272 | bytes 22413904 | solution.py:104
  85.6 1.2 fusion.226
  92.0 1.2 fusion.227
  93.2 1.2 convolution_subtract_fusion.5
  94.4 1.2 fusion.226
  103.3 1.2 fusion.226
  112.1 1.2 fusion.226
  121.0 1.2 fusion.226
  129.8 1.2 fusion.226
  138.7 1.2 fusion.226
  147.6 1.2 fusion.226
  162.8 1.2 fusion.227
  165.3 1.2 fusion.226
  171.6 1.2 fusion.227
  174.1 1.2 fusion.226
  188.5 27.1 %copy.40 = bf16[12,16,8192]{1,0,2:T(8,128)(2,1)} copy(bf16[12,16,8192]{2,1,0:T(8,128)(2,1)} %get-tuple-element.79) | data formatting | bytes 6291456 | tf_op jit(solution)/shard_map/while | solution.py:104
  215.6 34.8 %reshape.73 = bf16[64,2,12288]{2,1,0:T(2,128)(2,1)S(1)} reshape(bf16[8192,12,16]{2,1,0:T(8,128)(2,1)} %bitcast.118) | data formatting | bytes 6291456
  250.4 71.3 %all_to_all.38 = bf16[64,2,12288]{2,1,0:T(2,128)(2,1)} all-to-all(bf16[64,2,12288]{2,1,0:T(2,128)(2,1)S(1)} %reshape.73), channel_id=1, replica_groups=mesh['seq'=64,'dp'=4] {'seq'}, dimensions={0} | all-to-all | bytes 6291456 | tf_op jit(solution)/shard_map/all_to_all | solution.py:105
  321.7 34.0 %reshape.74 = bf16[8192,12,16]{2,1,0:T(8,128)(2,1)} reshape(bf16[64,2,12288]{2,1,0:T(2,128)(2,1)} %all_to_all.38) | data formatting | bytes 6291456
  355.7 28.9 %copy.42 = bf16[12,64,16,128]{3,2,1,0:T(8,128)(2,1)S(1)} copy(bf16[12,64,16,128]{2,0,3,1:T(8,128)(2,1)} %bitcast.119) | data formatting | bytes 6291456 | tf_op jit(solution)/shard_map/all_to_all | solution.py:105
  384.6 10.7 %fusion.89 = bf16[128,1024]{1,0:T(8,128)(2,1)} fusion(bf16[12,1024,128]{2,1,0:T(8,128)(2,1)S(1)} %bitcast.120, bf16[12,1024,1024]{2,1,0:T(8,128)(2,1)} %all-gather.2.cloned.1.call-done, bf16[128,1024]{1,0:T(8,128)(2,1)S(1)} %copy-done), kind=kOutput, calls=%fused_computation.102 | convolution fusion | flops 3221618688 | bytes 28835840 | tf_op jit(solution)/shard_map/kct,kcd->td/dot_general | solution.py:106
  (128 shorter events, 98.1 us)
Async XLA Ops:
  6.5 378.1 %all-gather.2.cloned.1.call-start = ((), (), s32[]{:S(2)}) async-start(), calls=%async_computation.3 | async-start | bytes 25559040 | tf_op jit(solution)/shard_map/all_gather | solution.py:109
  10.3 30.9 %all-to-all-start.1 = ((bf16[128,64,16]{0,2,1:T(8,128)(2,1)}), bf16[128,64,16]{0,2,1:T(8,128)(2,1)S(1)}, u32[]{:S(2)}, u32[]{:S(2)}) async-start(bf16[128,64,16]{0,2,1:T(8,128)(2,1)} %bitcast.7), calls=%async_computation.1 | async-start | bytes 524288 | tf_op jit(solution)/shard_map/all_to_all | solution.py:93
  42.7 32.3 %all-to-all-start = ((f32[64,12,128]{2,1,0:T(8,128)}), f32[64,12,128]{2,1,0:T(8,128)S(1)}, u32[]{:S(2)}, u32[]{:S(2)}) async-start(f32[64,12,128]{2,1,0:T(8,128)} %stack.2), calls=%async_computation | async-start | bytes 1048576 | tf_op jit(solution)/shard_map/all_to_all | solution.py:14
  355.7 28.9 %copy-start = (bf16[128,1024]{1,0:T(8,128)(2,1)S(1)}, bf16[128,1024]{1,0:T(8,128)(2,1)}, u32[]{:S(2)}) copy-start(bf16[128,1024]{1,0:T(8,128)(2,1)} %param.6) | copy-start | bytes 786436
Sparse Core Ops, SparseCore 0:
  10.7 240.8 all-gather.1
